TPU v7x, 512 devices: a whole 4x8x8 slice. The times are simulated.
512 devices in a mesh: expert: 64 (over y, z), dp: 8 (over x, core).
Axes of the slice: x: 4, y: 8, z: 8, core: 2. Of those that a mesh axis runs over, the one named last changes fastest.
Arguments:
- tokens: bfloat16 [8192, 3584], P(('dp', 'expert')), parts along dimension 0, may hold values from -6 to 6
- expert_ids: int32 [8192, 2], P(('dp', 'expert')), parts along dimension 0, may hold values from 0 to 5, as said below
- gate_weights: float32 [8192, 2], P(('dp', 'expert')), parts along dimension 0, may hold values from 0.1 to 1
- replica_pick: int32 [8192, 2], P(('dp', 'expert')), parts along dimension 0, may hold values from 0 to 1
- placement: int32 [8], replicated, may hold values from 0 to 5, as said below
- w_in: bfloat16 [2, 3584, 8192], P(None, None, 'expert')
- w_out: bfloat16 [8192, 3584], P('expert')
Outputs:
- moe_out: bfloat16 [8192, 3584], P(('dp', 'expert')), parts along dimension 0
There are 8 independent parts, one for each index of `dp`. A program takes and returns all parts, laid end to end along the dimension named above; an argument that names none is the same for every part. Nothing has to cross between parts.
Inputs may be any that keep to these rules, and one draw needn't show every extreme that they name: `expert_ids`: each row names 2 different experts. `placement`: every expert is named once or twice, 2 of them twice, at any positions.
All inputs are finite; a program needn't handle non-finite values.
Results may differ from a plain program's by a relative error of at most 0.012.
Values may be sent and summed in bfloat16 or wider, within the bound.
A program may use at most 64 MiB of HBM per device.

v0:
```python
import jax
import jax.numpy as jnp
from jax import lax
from jax.sharding import PartitionSpec as P


def route_block(expert_ids, replica_pick, gate_weights, placement, slot_count, capacity):
    tok_count, top_count = expert_ids.shape
    copy_index = jnp.arange(slot_count, dtype=jnp.int32)
    same_expert = placement[:, None] == placement[None, :]
    before = jnp.sum(
        (same_expert & (copy_index[:, None] < copy_index[None, :])).astype(jnp.int32), axis=0
    )
    matches = placement[None, None, :] == expert_ids[:, :, None]
    copies = jnp.sum(matches.astype(jnp.int32), axis=-1)
    wanted = replica_pick % copies
    chosen = (matches & (before[None, None, :] == wanted[:, :, None])).astype(jnp.int32)
    flat_hot = chosen.reshape(tok_count * top_count, slot_count)
    earlier = jnp.cumsum(flat_hot, axis=0) - flat_hot
    slot_rank = jnp.sum(earlier * flat_hot, axis=-1).reshape(tok_count, top_count)
    slot_index = jnp.arange(capacity, dtype=jnp.int32)
    in_slot = chosen[:, :, :, None] * (
        slot_rank[:, :, None, None] == slot_index[None, None, None, :]
    ).astype(jnp.int32)
    in_slot = in_slot.astype(jnp.float32)
    pick_rows = jnp.sum(in_slot, axis=1).reshape(tok_count, slot_count * capacity).T
    combine_rows = jnp.sum(in_slot * gate_weights[:, :, None, None], axis=1).reshape(
        tok_count, slot_count * capacity
    )
    return (pick_rows, combine_rows)


def body(tokens, expert_ids, gate_weights, replica_pick, placement, w_in, w_out):
    n_devices = lax.axis_size("expert")
    group_size = min(8, n_devices // 4)
    slot_count = n_devices // group_size
    tok_count, model_width = tokens.shape
    capacity = tok_count * expert_ids.shape[1] // slot_count
    pick_rows, combine_rows = route_block(
        expert_ids, replica_pick, gate_weights, placement, slot_count, capacity
    )
    slot_rows = jnp.dot(
        pick_rows.astype(jnp.bfloat16), tokens, preferred_element_type=jnp.float32
    ).astype(jnp.bfloat16)
    slot_rows = slot_rows.reshape(slot_count, capacity, model_width)
    send_rows = jnp.broadcast_to(
        slot_rows[:, None], (slot_count, group_size, capacity, model_width)
    )
    send_rows = send_rows.reshape(n_devices, capacity, model_width)
    received = lax.all_to_all(send_rows, "expert", split_axis=0, concat_axis=0, tiled=True)
    senders, items, _ = received.shape
    flat_rows = received.reshape(senders * items, model_width)
    gate_up = jnp.einsum("rd,gdf->grf", flat_rows, w_in, preferred_element_type=jnp.float32)
    hidden = (jax.nn.silu(gate_up[0]) * gate_up[1]).astype(jnp.bfloat16)
    partial_value = jnp.dot(hidden, w_out, preferred_element_type=jnp.float32).astype(jnp.bfloat16)
    partial_value = partial_value.reshape(senders, items, model_width)
    returned = lax.all_to_all(partial_value, "expert", split_axis=0, concat_axis=0, tiled=True)
    expert_out = jnp.sum(
        returned.reshape(slot_count, group_size, capacity, model_width).astype(jnp.float32), axis=1
    )
    expert_out = expert_out.reshape(slot_count * capacity, model_width)
    moe_out = jnp.dot(combine_rows, expert_out, preferred_element_type=jnp.float32)
    return moe_out.astype(jnp.bfloat16)


def solution(mesh):
    in_specs = (
        P(("dp", "expert"), None),
        P(("dp", "expert"), None),
        P(("dp", "expert"), None),
        P(("dp", "expert"), None),
        P(),
        P(None, None, "expert"),
        P("expert", None),
    )
    out_specs = P(("dp", "expert"), None)
    return jax.shard_map(body, mesh=mesh, in_specs=in_specs, out_specs=out_specs, check_vma=False)
```

profile of v0, /device:TPU:6, one launch (start us, length us, event | category | flops | bytes accessed | tf_op | source)
XLA Modules:
  0.0 140.1 jit_solution(4358948706646139995)
XLA Ops:
  0.0 0.9 convert_reduce_fusion.2
  0.9 0.8 fusion.7
  1.7 0.8 copy.24
  2.4 0.8 and_select_fusion
  3.2 0.1 copy.25
  3.3 0.1 eq.104
  3.4 0.8 fusion.8
  4.1 0.1 eq.100
  4.2 0.7 fusion.6
  5.0 0.8 select_reduce_fusion
  5.9 0.1 eq.107
  5.9 0.1 copy.26
  6.0 0.7 convert_reduce_fusion.1
  6.8 1.1 convolution_convert_fusion.1
  7.9 0.1 broadcast_in_dim.9
  7.9 0.5 broadcast_in_dim.10
  8.4 62.9 %all_to_all.10 = bf16[64,4,3584]{2,1,0:T(4,128)(2,1)} all-to-all(bf16[64,4,3584]{2,1,0:T(4,128)(2,1)S(1)} %bitcast.29), channel_id=1, replica_groups=mesh['expert'=64,'dp'=8] {'expert'}, dimensions={0} | all-to-all | bytes 3670016 | tf_op jit(solution)/shard_map/all_to_all | solution.py:50
  71.3 3.9 %reshape.45 = bf16[256,3584,1]{1,0,2:T(8,128)(2,1)} reshape(bf16[64,4,3584]{2,1,0:T(4,128)(2,1)} %all_to_all.10) | data formatting | bytes 3670016 | tf_op jit(solution)/shard_map/reshape | solution.py:52
  75.2 2.2 %convolution_bitcast_fusion.1 = f32[2,256,128]{2,1,0:T(8,128)S(1)} fusion(bf16[256,3584,1]{1,0,2:T(8,128)(2,1)} %reshape.45, bf16[2,3584,128]{2,1,0:T(8,128)(2,1)S(1)} %copy-done), kind=kOutput, calls=%fused_computation.5 | convolution fusion | flops 469762048 | bytes 3932160 | tf_op jit(solution)/shard_map/rd,gdf->grf/dot_general | solution.py:53
  77.5 1.9 %convolution_convert_fusion = bf16[256,3584]{1,0:T(8,128)(2,1)} fusion(bf16[128,3584]{1,0:T(8,128)(2,1)S(1)} %copy-done.1, f32[2,256,128]{2,1,0:T(8,128)S(1)} %convolution_bitcast_fusion.1), kind=kOutput, calls=%fused_computation | convolution fusion | flops 235995136 | bytes 3014656 | tf_op jit(solution)/shard_map/dot_general | solution.py:55
  79.3 4.1 %reshape.43 = bf16[64,4,3584]{2,1,0:T(4,128)(2,1)} reshape(bf16[256,3584]{1,0:T(8,128)(2,1)} %convolution_convert_fusion) | data formatting | bytes 3670016 | tf_op jit(solution)/shard_map/reshape | solution.py:56
  83.4 55.0 %all_to_all.11 = bf16[64,4,3584]{2,1,0:T(4,128)(2,1)S(1)} all-to-all(bf16[64,4,3584]{2,1,0:T(4,128)(2,1)} %reshape.43), channel_id=1, replica_groups=mesh['expert'=64,'dp'=8] {'expert'}, dimensions={0} | all-to-all | bytes 3670016 | tf_op jit(solution)/shard_map/all_to_all | solution.py:57
  138.4 0.8 convert_reduce_fusion
  139.2 0.9 fusion
  (7 shorter events, 0.1 us)
Async XLA Ops:
  0.0 75.2 %copy-start = (bf16[2,3584,128]{2,1,0:T(8,128)(2,1)S(1)}, bf16[2,3584,128]{2,1,0:T(8,128)(2,1)}, u32[]{:S(2)}) copy-start(bf16[2,3584,128]{2,1,0:T(8,128)(2,1)} %param.12) | copy-start | bytes 5505028
  75.2 2.2 %copy-start.1 = (bf16[128,3584]{1,0:T(8,128)(2,1)S(1)}, bf16[128,3584]{1,0:T(8,128)(2,1)}, u32[]{:S(2)}) copy-start(bf16[128,3584]{1,0:T(8,128)(2,1)} %param.13) | copy-start | bytes 2752516
where the time goes:
time: 142 us; the launch traced here: 140 us
  blocking collectives  118 us (83%)
  local copies, waits for them, and re-layouts  9.7 us (7%)
  other arithmetic  6.38 us (4%)
  matrix products  6.06 us (4%)
    all_to_all x1, blocking collectives, body(): lax.all_to_all(send_rows, 'expert', split_axis=0, concat_axis=0, tiled=True)  62.9 us
    all_to_all x1, blocking collectives, body(): lax.all_to_all(partial_value, 'expert', split_axis=0, concat_axis=0, tile...  55 us
    reshape x1, local copies, waits for them, and re-layouts, body(): partial_value = partial_value.reshape(senders, items, model_width)  4.06 us
    reshape x1, local copies, waits for them, and re-layouts, body(): flat_rows = received.reshape(senders * items, model_width)  3.91 us

commit v1 on v0

v1 whole, which is shorter than its diff:
```python
import functools

import jax
import jax.numpy as jnp
from jax import lax
from jax.experimental import pallas as pl
from jax.experimental.pallas import tpu as pltpu
from jax.sharding import PartitionSpec as P

N = 8
OFFS = (0, 1, -1, 2, -2, 3, -3, 4)
FOLD = 4
CAP = 4
ROWS = FOLD * CAP
MESH = pl.DeviceIdType.MESH
F32 = jnp.float32
BF16 = jnp.bfloat16
FAR = ((0, 1), (2, 3))


def iota(shape, axis):
    return lax.broadcasted_iota(jnp.int32, shape, axis)


def routing(y, ids_ref, gw_ref, pick_ref, place_ref, pad):
    tok = ids_ref.shape[1]
    pad[...] = jnp.zeros_like(pad)
    pad[0:2, 0:tok] = ids_ref[...].astype(F32)
    pad[2:4, 0:tok] = pick_ref[...].astype(F32)
    pad[4:6, 0:tok] = gw_ref[...]
    pad[8:9, 0:N] = place_ref[...].astype(F32)
    wide = pad[0:8, :]
    wide = (
        wide
        + pltpu.roll(wide, tok, 1)
        + pltpu.roll(wide, 2 * tok, 1)
        + pltpu.roll(wide, 3 * tok, 1)
    )
    place_row = jnp.broadcast_to(pad[8:9, :], (N, 128))
    sub, lane = iota((N, 128), 0), iota((N, 128), 1)
    place_col = jnp.sum(jnp.where(sub == lane, place_row, 0.0), axis=1, keepdims=True)
    before = jnp.sum(
        jnp.where((place_row == place_col) & (lane < sub), 1.0, 0.0), axis=1, keepdims=True
    )
    subf = sub.astype(F32)
    row, col = iota((128, 128), 0), iota((128, 128), 1)
    j = row // ROWS
    offs = jnp.where(j % 2 == 1, (j + 1) // 2, -(j // 2))
    copy_of_row = ((y - offs + N) % N).astype(F32)
    chosen = []
    for k in range(2):
        match = place_col == wide[k : k + 1, :]
        copies = jnp.sum(jnp.where(match, 1.0, 0.0), axis=0, keepdims=True)
        wanted = jnp.where(copies > 1.5, wide[2 + k : 3 + k, :], 0.0)
        phys = jnp.sum(
            jnp.where(match & (before == wanted), subf, 0.0), axis=0, keepdims=True
        )
        chosen.append(jnp.where(copy_of_row == phys, 1.0, 0.0))
    earlier = jnp.where((row // tok == col // tok) & (row < col), 1.0, 0.0).astype(BF16)
    rank = jnp.dot((chosen[0] + chosen[1]).astype(BF16), earlier, preferred_element_type=F32)
    own = col // tok == (row // CAP) % FOLD
    slot = (row % CAP).astype(F32)
    in0 = jnp.where(own & (rank == slot), chosen[0], 0.0)
    in1 = jnp.where(own & (rank + chosen[0] == slot), chosen[1], 0.0)
    pick = (in0 + in1).astype(BF16)
    combine = in0 * wide[4:5, :] + in1 * wide[5:6, :]
    return pick, combine.T


def kernel(
    ids_ref, gw_ref, pick_ref, place_ref, tok_ref, win_ref, wout_ref, out_ref,
    pad, w1, w2, comb, ybuf, xbuf, xrows, part, sbuf, rbuf, obuf, cbuf,
    wsem, yds, ydr, ags, agr, rss, rsr, yrs, yrr,
):
    wide = tok_ref.shape[1] // FOLD
    units = w2.shape[0]
    e = lax.axis_index("expert")
    y, z = e // N, e % N
    right = y * N + (z + 1) % N
    left = y * N + (z + N - 1) % N
    side = (right, left)

    loads = [
        pltpu.make_async_copy(win_ref.at[0], w1.at[:, 0:units], wsem.at[0]),
        pltpu.make_async_copy(win_ref.at[1], w1.at[:, units : 2 * units], wsem.at[1]),
        pltpu.make_async_copy(wout_ref, w2, wsem.at[2]),
    ]
    for load in loads:
        load.start()

    barrier = pltpu.get_barrier_semaphore()
    peers = [(y + d) % N * N + z for d in range(1, N)] + [right, left]
    for peer in peers:
        pl.semaphore_signal(barrier, inc=1, device_id={"expert": peer}, device_id_type=MESH)

    pick, combine = routing(y, ids_ref, gw_ref, pick_ref, place_ref, pad)
    tok_fold = jnp.concatenate(
        [tok_ref[:, q * wide : (q + 1) * wide] for q in range(FOLD)], axis=0
    )
    messages = jnp.dot(
        pick[:, : tok_fold.shape[0]], tok_fold, preferred_element_type=F32
    ).astype(BF16)
    ybuf[...] = messages
    xbuf[0, 0, 0:ROWS, :] = messages[0:ROWS]
    half_rows = combine[: tok_fold.shape[0]]
    high = half_rows.astype(BF16)
    comb[...] = jnp.concatenate([high, (half_rows - high.astype(F32)).astype(BF16)], axis=0)

    pl.semaphore_wait(barrier, len(peers))

    def remote(src, dst, send, recv, target):
        return pltpu.make_async_remote_copy(
            src_ref=src, dst_ref=dst, send_sem=send, recv_sem=recv,
            device_id={"expert": target}, device_id_type=MESH,
        )

    def msg(i):
        return slice(i * ROWS, (i + 1) * ROWS)

    sends = []

    y_in = {}
    for j in range(1, N):
        copy = remote(
            ybuf.at[msg(j)], xbuf.at[j // 4, 0, msg(j % 4)], yds.at[j], ydr.at[j],
            (y - OFFS[j] + N) % N * N + z,
        )
        copy.start()
        sends.append(copy)
        y_in[j] = copy

    gather = {}

    def gather_step(h, s):
        for i in range(4):
            for d in range(2):
                if s == 0:
                    if d == 0 and h * 4 + i > 0:
                        y_in[h * 4 + i].wait_recv()
                else:
                    gather[h, d, s - 1, i].wait_recv()
                if s == 3 and i not in FAR[d]:
                    continue
                src = (N - s) % N if d == 0 else s
                dst = N - 1 - s if d == 0 else s + 1
                copy = remote(
                    xbuf.at[h, src, msg(i)], xbuf.at[h, dst, msg(i)],
                    ags.at[h, d, s, i], agr.at[h, d, s, i], side[d],
                )
                copy.start()
                sends.append(copy)
                gather[h, d, s, i] = copy

    a, b = iota((4 * ROWS, 4 * ROWS), 0), iota((4 * ROWS, 4 * ROWS), 1)
    swap = jnp.where(
        (a // 16 == (b // 4) % 4) & ((a // 4) % 4 == b // 16) & (a % 4 == b % 4), 1.0, 0.0
    ).astype(BF16)

    def unfold(h, slot):
        rows = jnp.dot(swap, xbuf[h, slot], preferred_element_type=F32).astype(BF16)
        for q in range(FOLD):
            xrows[h, slot * ROWS : (slot + 1) * ROWS, q * wide : (q + 1) * wide] = rows[msg(q)]

    def hidden_of(h):
        gate_up = jnp.dot(xrows[h], w1[...], preferred_element_type=F32)
        gate = gate_up[:, :units]
        return (gate / (1.0 + jnp.exp(-gate)) * gate_up[:, units:]).astype(BF16)

    def down(h, hidden):
        for q in range(FOLD):
            part[h, q] = jnp.dot(
                hidden, w2[:, q * wide : (q + 1) * wide], preferred_element_type=F32
            )

    reduce = {}

    def reduce_step(h, s):
        for fresh in (True, False):
            for q in range(FOLD):
                for d in range(2):
                    known = s > 0 and (s > 1 or q in FAR[d])
                    if known == fresh or (s == 0 and q not in FAR[d]):
                        continue
                    slot = 4 - s if d == 0 else 4 + s
                    value = part[h, q, slot * ROWS : (slot + 1) * ROWS, :]
                    if known:
                        reduce[h, d, s - 1, q].wait_recv()
                        value = value + rbuf[h, d, s - 1, q].astype(F32)
                    sbuf[h, d, s, q] = value.astype(BF16)
                    copy = remote(
                        sbuf.at[h, d, s, q], rbuf.at[h, d, s, q],
                        rss.at[h, d, s, q], rsr.at[h, d, s, q], side[d],
                    )
                    copy.start()
                    sends.append(copy)
                    reduce[h, d, s, q] = copy

    back = {}

    def finish(h):
        sums = []
        for q in range(FOLD):
            value = part[h, q, 0:ROWS, :]
            for d in range(2):
                reduce[h, d, 3, q].wait_recv()
                value = value + rbuf[h, d, 3, q].astype(F32)
            sums.append(value.astype(BF16))
        folded = jnp.dot(
            swap, jnp.concatenate(sums, axis=0), preferred_element_type=F32
        ).astype(BF16)
        obuf[h] = folded
        for i in reversed(range(4)):
            j = h * 4 + i
            if j == 0:
                cbuf[0:ROWS, :] = folded[0:ROWS]
                continue
            copy = remote(
                obuf.at[h, msg(i)], cbuf.at[msg(j)], yrs.at[j], yrr.at[j],
                (y + OFFS[j] + N) % N * N + z,
            )
            copy.start()
            sends.append(copy)
            back[j] = copy

    def gather_last(h):
        for d in range(2):
            for i in FAR[d]:
                gather[h, d, 3, i].wait_recv()

    for s in range(4):
        gather_step(0, s)
        unfold(0, (N - s) % N)
        if s > 0:
            unfold(0, s)
    gather_step(1, 0)
    unfold(1, 0)
    gather_last(0)
    unfold(0, 4)
    loads[0].wait()
    loads[1].wait()
    gather_step(1, 1)
    hidden0 = hidden_of(0)
    unfold(1, 7)
    unfold(1, 1)
    gather_step(1, 2)
    loads[2].wait()
    down(0, hidden0)
    unfold(1, 6)
    unfold(1, 2)
    gather_step(1, 3)
    reduce_step(0, 0)
    unfold(1, 5)
    unfold(1, 3)
    reduce_step(0, 1)
    gather_last(1)
    unfold(1, 4)
    hidden1 = hidden_of(1)
    reduce_step(0, 2)
    down(1, hidden1)
    reduce_step(0, 3)
    reduce_step(1, 0)
    reduce_step(1, 1)
    finish(0)
    reduce_step(1, 2)
    reduce_step(1, 3)
    finish(1)
    for j in range(1, N):
        back[j].wait_recv()
    both = jnp.dot(comb[...], cbuf[...], preferred_element_type=F32)
    half = both.shape[0] // 2
    result = both[:half] + both[half:]
    tok = out_ref.shape[0]
    for q in range(FOLD):
        out_ref[:, q * wide : (q + 1) * wide] = result[q * tok : (q + 1) * tok].astype(BF16)
    for copy in sends:
        copy.wait_send()


def body(tokens, expert_ids, gate_weights, replica_pick, placement, w_in, w_out):
    tok, width = tokens.shape
    units = w_out.shape[0]
    wide = width // FOLD
    vmem = pl.BlockSpec(memory_space=pltpu.VMEM)
    anywhere = pl.BlockSpec(memory_space=pl.ANY)
    dma = pltpu.SemaphoreType.DMA
    return pl.pallas_call(
        kernel,
        out_shape=jax.ShapeDtypeStruct((tok, width), BF16),
        in_specs=[vmem] * 5 + [anywhere] * 2,
        out_specs=vmem,
        scratch_shapes=[
            pltpu.VMEM((16, 128), F32),
            pltpu.VMEM((width, 2 * units), BF16),
            pltpu.VMEM((units, width), BF16),
            pltpu.VMEM((2 * FOLD * tok, 128), BF16),
            pltpu.VMEM((N * ROWS, wide), BF16),
            pltpu.VMEM((2, N, 4 * ROWS, wide), BF16),
            pltpu.VMEM((2, N * ROWS, width), BF16),
            pltpu.VMEM((2, FOLD, N * ROWS, wide), F32),
            pltpu.VMEM((2, 2, 4, FOLD, ROWS, wide), BF16),
            pltpu.VMEM((2, 2, 4, FOLD, ROWS, wide), BF16),
            pltpu.VMEM((2, 4 * ROWS, wide), BF16),
            pltpu.VMEM((N * ROWS, wide), BF16),
            dma((3,)),
            dma((N,)),
            dma((N,)),
            dma((2, 2, 4, 4)),
            dma((2, 2, 4, 4)),
            dma((2, 2, 4, 4)),
            dma((2, 2, 4, 4)),
            dma((N,)),
            dma((N,)),
        ],
        compiler_params=pltpu.CompilerParams(collective_id=0, has_side_effects=True),
    )(
        expert_ids.T, gate_weights.T, replica_pick.T, placement.reshape(1, -1),
        tokens, w_in, w_out,
    )


def solution(mesh):
    in_specs = (
        P(("dp", "expert"), None),
        P(("dp", "expert"), None),
        P(("dp", "expert"), None),
        P(("dp", "expert"), None),
        P(),
        P(None, None, "expert"),
        P("expert", None),
    )
    out_specs = P(("dp", "expert"), None)
    return jax.shard_map(body, mesh=mesh, in_specs=in_specs, out_specs=out_specs, check_vma=False)
```

time: 142 us -> 78.1 us (0.55)
  blocking collectives: 118 us -> 0 us
  Pallas kernels: 0 us -> 75.9 us
  local copies, waits for them, and re-layouts: 9.7 us -> 1.55 us
  other arithmetic: 6.38 us -> 0 us
  matrix products: 6.06 us -> 0 us
    all_to_all x2 -> x0, blocking collectives: 118 us -> none  [the longest x1 62.9 us: body(): lax.all_to_all(send_rows, 'expert', split_axis=0, concat_axis=0, tiled=True)]
    pallas_call x0 -> x1, Pallas kernels: none -> 75.9 us  [body(): pl.pallas_call(kernel, out_shape=jax.ShapeDtypeStruct((tok, width), BF16)...]
    reshape x2 -> x0, local copies, waits for them, and re-layouts: 7.97 us -> none  [the longest x1 4.06 us: body(): partial_value = partial_value.reshape(senders, items, model_width)]
    dot_general x4 -> x0, matrix products: 6.06 us -> none  [the longest x1 2.22 us: body(): jnp.einsum('rd,gdf->grf', flat_rows, w_in, preferred_element_type=jnp.flo...]
    reduce_sum x5 -> x0, other arithmetic: 4.03 us -> none  [the longest x1 0.89 us: route_block(): jnp.sum((same_expert & (copy_index[:, None] < copy_index[None, :])).astyp...]
    convert_element_type x3 -> x0, other arithmetic: 1.49 us -> none  [the longest x2 1.49 us: route_block(): (matches & (before[None, None, :] == wanted[:, :, None])).astype(jnp.int32)]
where the time goes in v1:
time: 78.1 us; the launch traced here: 77.5 us
  Pallas kernels  75.9 us (97%)
  local copies, waits for them, and re-layouts  1.55 us (2%)
    pallas_call x1, Pallas kernels, body(): pl.pallas_call(kernel, out_shape=jax.ShapeDtypeStruct((tok, width), BF16)...  75.9 us

profile of v1, /device:TPU:6, one launch (start us, length us, event | category | flops | bytes accessed | tf_op | source)
XLA Modules:
  0.0 77.5 jit_solution(4018452451390740764)
XLA Ops:
  0.0 75.9 %shard_map.73 = bf16[16,3584]{1,0:T(8,128)(2,1)} custom-call(s32[2,16]{1,0:T(2,128)} %bitcast.4, f32[2,16]{1,0:T(2,128)} %bitcast.5, s32[2,16]{1,0:T(2,128)} %bitcast.6, s32[1,8]{1,0:T(1,128)} %bitcast.7, bf16[16,3584]{1,0:T(8,128)(2,1)} %tok_ref.1, bf16[2,3584,128]{2,1,0:T(8,128)(2,1)} %win_ref.1, bf16[128,3584]{1,0:T(8,128)(2,1)} %wout_ref.1), custom_call_target="tpu_custom_call" | custom-call | tf_op jit(solution)/shard_map/pallas_call | solution.py:286
  76.0 1.6 %copy.9 = bf16[16,3584]{1,0:T(8,128)(2,1)} copy(bf16[16,3584]{1,0:T(8,128)(2,1)} %shard_map.73) | data formatting | bytes 229376

commit v2 on v1

--- a/solution.py
+++ b/solution.py
@@ -16,6 +16,7 @@
 F32 = jnp.float32
 BF16 = jnp.bfloat16
 FAR = ((0, 1), (2, 3))
+Y_TIME = (0.0, 2.5, 2.5, 3.3, 3.4, 4.2, 4.2, 5.0)
 
 
 def iota(shape, axis):
@@ -70,7 +71,7 @@
 def kernel(
     ids_ref, gw_ref, pick_ref, place_ref, tok_ref, win_ref, wout_ref, out_ref,
     pad, w1, w2, comb, ybuf, xbuf, xrows, part, sbuf, rbuf, obuf, cbuf,
-    wsem, yds, ydr, ags, agr, rss, rsr, yrs, yrr,
+    wsem, sent, ydr, agr, agl, rsr, rsl, yrr,
 ):
     wide = tok_ref.shape[1] // FOLD
     units = w2.shape[0]
@@ -117,39 +118,38 @@
     def msg(i):
         return slice(i * ROWS, (i + 1) * ROWS)
 
-    sends = []
-
     y_in = {}
     for j in range(1, N):
-        copy = remote(
-            ybuf.at[msg(j)], xbuf.at[j // 4, 0, msg(j % 4)], yds.at[j], ydr.at[j],
+        y_in[j] = remote(
+            ybuf.at[msg(j)], xbuf.at[j // 4, 0, msg(j % 4)], sent.at[0], ydr.at[j],
             (y - OFFS[j] + N) % N * N + z,
         )
-        copy.start()
-        sends.append(copy)
-        y_in[j] = copy
+        y_in[j].start()
 
     gather = {}
 
-    def gather_step(h, s):
-        for i in range(4):
-            for d in range(2):
-                if s == 0:
-                    if d == 0 and h * 4 + i > 0:
-                        y_in[h * 4 + i].wait_recv()
-                else:
-                    gather[h, d, s - 1, i].wait_recv()
-                if s == 3 and i not in FAR[d]:
-                    continue
-                src = (N - s) % N if d == 0 else s
-                dst = N - 1 - s if d == 0 else s + 1
-                copy = remote(
-                    xbuf.at[h, src, msg(i)], xbuf.at[h, dst, msg(i)],
-                    ags.at[h, d, s, i], agr.at[h, d, s, i], side[d],
-                )
-                copy.start()
-                sends.append(copy)
-                gather[h, d, s, i] = copy
+    def gather_one(s, m):
+        h, i = m // 4, m % 4
+        if s == 0 and m > 0:
+            y_in[m].wait_recv()
+        for d in range(2):
+            if s > 0:
+                gather[h, d, s - 1, i].wait_recv()
+            if s == 3 and i not in FAR[d]:
+                continue
+            src = (N - s) % N if d == 0 else s
+            dst = N - 1 - s if d == 0 else s + 1
+            copy = remote(
+                xbuf.at[h, src, msg(i)], xbuf.at[h, dst, msg(i)], sent.at[1],
+                agr.at[h, d, s, i] if s < 3 else agl.at[h, d], side[d],
+            )
+            copy.start()
+            gather[h, d, s, i] = copy
+
+    def gather_last(h):
+        for d in range(2):
+            rows = xbuf.at[h, 4, FAR[d][0] * ROWS : (FAR[d][1] + 1) * ROWS]
+            remote(rows, rows, sent.at[1], agl.at[h, d], side[d]).wait_recv()
 
     a, b = iota((4 * ROWS, 4 * ROWS), 0), iota((4 * ROWS, 4 * ROWS), 1)
     swap = jnp.where(
@@ -174,106 +174,93 @@
 
     reduce = {}
 
-    def reduce_step(h, s):
-        for fresh in (True, False):
-            for q in range(FOLD):
+    def place(d, s, q):
+        return FAR[d].index(q) if s == 0 else 4 * s - 2 + q
+
+    def reduce_stage(h, stage):
+        for far in (True, False):
+            s = stage if far else stage + 1
+            if s > 3:
+                continue
+            for n in range(2):
                 for d in range(2):
-                    known = s > 0 and (s > 1 or q in FAR[d])
-                    if known == fresh or (s == 0 and q not in FAR[d]):
-                        continue
+                    q = FAR[d if far else 1 - d][n]
                     slot = 4 - s if d == 0 else 4 + s
                     value = part[h, q, slot * ROWS : (slot + 1) * ROWS, :]
-                    if known:
+                    if stage > 0:
                         reduce[h, d, s - 1, q].wait_recv()
-                        value = value + rbuf[h, d, s - 1, q].astype(F32)
-                    sbuf[h, d, s, q] = value.astype(BF16)
+                        value = value + rbuf[h, d, place(d, s - 1, q)].astype(F32)
+                    at = place(d, s, q)
+                    sbuf[h, d, at] = value.astype(BF16)
                     copy = remote(
-                        sbuf.at[h, d, s, q], rbuf.at[h, d, s, q],
-                        rss.at[h, d, s, q], rsr.at[h, d, s, q], side[d],
+                        sbuf.at[h, d, at], rbuf.at[h, d, at], sent.at[2],
+                        rsr.at[h, d, at] if s < 3 else rsl.at[h, d], side[d],
                     )
                     copy.start()
-                    sends.append(copy)
                     reduce[h, d, s, q] = copy
 
-    back = {}
-
     def finish(h):
+        for d in range(2):
+            last = rbuf.at[h, d, 10:14]
+            remote(last, last, sent.at[2], rsl.at[h, d], side[d]).wait_recv()
         sums = []
         for q in range(FOLD):
             value = part[h, q, 0:ROWS, :]
             for d in range(2):
-                reduce[h, d, 3, q].wait_recv()
-                value = value + rbuf[h, d, 3, q].astype(F32)
+                value = value + rbuf[h, d, 10 + q].astype(F32)
             sums.append(value.astype(BF16))
         folded = jnp.dot(
             swap, jnp.concatenate(sums, axis=0), preferred_element_type=F32
         ).astype(BF16)
-        obuf[h] = folded
+        obuf[4 * h * ROWS : 4 * (h + 1) * ROWS] = folded
         for i in reversed(range(4)):
             j = h * 4 + i
             if j == 0:
                 cbuf[0:ROWS, :] = folded[0:ROWS]
                 continue
-            copy = remote(
-                obuf.at[h, msg(i)], cbuf.at[msg(j)], yrs.at[j], yrr.at[j],
+            remote(
+                obuf.at[msg(j)], cbuf.at[msg(j)], sent.at[3], yrr.at[0],
                 (y + OFFS[j] + N) % N * N + z,
-            )
-            copy.start()
-            sends.append(copy)
-            back[j] = copy
-
-    def gather_last(h):
-        for d in range(2):
-            for i in FAR[d]:
-                gather[h, d, 3, i].wait_recv()
-
-    for s in range(4):
-        gather_step(0, s)
-        unfold(0, (N - s) % N)
-        if s > 0:
-            unfold(0, s)
-    gather_step(1, 0)
-    unfold(1, 0)
-    gather_last(0)
-    unfold(0, 4)
+            ).start()
+
+    order = sorted(
+        (Y_TIME[m] + 4.0 * s, m, s) for s in range(4) for m in range(N)
+    )
+    done = {}
+    for _, m, s in order:
+        gather_one(s, m)
+        h = m // 4
+        done[h, s] = done.get((h, s), 0) + 1
+        if done[h, s] == 4:
+            unfold(h, (N - s) % N)
+            if s > 0:
+                unfold(h, s)
     loads[0].wait()
     loads[1].wait()
-    gather_step(1, 1)
-    hidden0 = hidden_of(0)
-    unfold(1, 7)
-    unfold(1, 1)
-    gather_step(1, 2)
     loads[2].wait()
-    down(0, hidden0)
-    unfold(1, 6)
-    unfold(1, 2)
-    gather_step(1, 3)
-    reduce_step(0, 0)
-    unfold(1, 5)
-    unfold(1, 3)
-    reduce_step(0, 1)
-    gather_last(1)
-    unfold(1, 4)
-    hidden1 = hidden_of(1)
-    reduce_step(0, 2)
-    down(1, hidden1)
-    reduce_step(0, 3)
-    reduce_step(1, 0)
-    reduce_step(1, 1)
+    for h in range(2):
+        gather_last(h)
+        unfold(h, 4)
+        hidden = hidden_of(h)
+        down(h, hidden)
+        reduce_stage(h, 0)
+    for stage in range(1, 4):
+        reduce_stage(0, stage)
+        reduce_stage(1, stage)
     finish(0)
-    reduce_step(1, 2)
-    reduce_step(1, 3)
     finish(1)
-    for j in range(1, N):
-        back[j].wait_recv()
+    others = cbuf.at[ROWS : N * ROWS]
+    remote(others, others, sent.at[3], yrr.at[0], right).wait_recv()
     both = jnp.dot(comb[...], cbuf[...], preferred_element_type=F32)
     half = both.shape[0] // 2
     result = both[:half] + both[half:]
     tok = out_ref.shape[0]
     for q in range(FOLD):
-        out_ref[:, q * wide : (q + 1) * wide] = result[q * tok : (q + 1) * tok].astype(BF16)
-    for copy in sends:
-        copy.wait_send()
+        out_ref[:, q * wide : (q + 1) * wide] = result[q * tok : (q + 1) * tok].astype(out_ref.dtype)
+    for sem, whole in (
+        (0, ybuf.at[ROWS : N * ROWS]), (1, xbuf.at[:, 0:7]), (2, sbuf), (3, obuf.at[ROWS : N * ROWS])
+    ):
+        remote(whole, whole, sent.at[sem], yrr.at[0], right).wait_send()
 
 
 def body(tokens, expert_ids, gate_weights, replica_pick, placement, w_in, w_out):
@@ -297,19 +284,18 @@
             pltpu.VMEM((2, N, 4 * ROWS, wide), BF16),
             pltpu.VMEM((2, N * ROWS, width), BF16),
             pltpu.VMEM((2, FOLD, N * ROWS, wide), F32),
-            pltpu.VMEM((2, 2, 4, FOLD, ROWS, wide), BF16),
-            pltpu.VMEM((2, 2, 4, FOLD, ROWS, wide), BF16),
-            pltpu.VMEM((2, 4 * ROWS, wide), BF16),
+            pltpu.VMEM((2, 2, 14, ROWS, wide), BF16),
+            pltpu.VMEM((2, 2, 14, ROWS, wide), BF16),
+            pltpu.VMEM((N * ROWS, wide), BF16),
             pltpu.VMEM((N * ROWS, wide), BF16),
             dma((3,)),
+            dma((4,)),
             dma((N,)),
-            dma((N,)),
-            dma((2, 2, 4, 4)),
-            dma((2, 2, 4, 4)),
-            dma((2, 2, 4, 4)),
-            dma((2, 2, 4, 4)),
-            dma((N,)),
-            dma((N,)),
+            dma((2, 2, 3, 4)),
+            dma((2, 2)),
+            dma((2, 2, 10)),
+            dma((2, 2)),
+            dma((1,)),
         ],
         compiler_params=pltpu.CompilerParams(collective_id=0, has_side_effects=True),
     )(

time: 78.1 us -> 65.6 us (0.84)
  Pallas kernels: 75.9 us -> 63.7 us
    pallas_call x1, Pallas kernels: 75.9 us -> 63.7 us  [body(): pl.pallas_call(kernel, out_shape=jax.ShapeDtypeStruct((tok, width), BF16)...]
where the time goes in v2:
time: 65.6 us; the launch traced here: 65.3 us
  Pallas kernels  63.7 us (97%)
  local copies, waits for them, and re-layouts  1.55 us (2%)
    pallas_call x1, Pallas kernels, body(): pl.pallas_call(kernel, out_shape=jax.ShapeDtypeStruct((tok, width), BF16)...  63.7 us
    unnamed x1, local copies, waits for them, and re-layouts  1.55 us

profile of v2, /device:TPU:6, one launch (start us, length us, event | category | flops | bytes accessed | tf_op | source)
XLA Modules:
  0.0 65.3 jit_solution(13922485359361282713)
XLA Ops:
  0.0 63.7 %shard_map.73 = bf16[16,3584]{1,0:T(8,128)(2,1)} custom-call(s32[2,16]{1,0:T(2,128)} %bitcast.4, f32[2,16]{1,0:T(2,128)} %bitcast.5, s32[2,16]{1,0:T(2,128)} %bitcast.6, s32[1,8]{1,0:T(1,128)} %bitcast.7, bf16[16,3584]{1,0:T(8,128)(2,1)} %tok_ref.1, bf16[2,3584,128]{2,1,0:T(8,128)(2,1)} %win_ref.1, bf16[128,3584]{1,0:T(8,128)(2,1)} %wout_ref.1), custom_call_target="tpu_custom_call" | custom-call | tf_op jit(solution)/shard_map/pallas_call | solution.py:273
  63.7 1.6 %copy.9 = bf16[16,3584]{1,0:T(8,128)(2,1)} copy(bf16[16,3584]{1,0:T(8,128)(2,1)} %shard_map.73) | data formatting | bytes 229376

commit v3 on v2

v3 whole, which is shorter than its diff:
```python
import functools

import jax
import jax.numpy as jnp
from jax import lax
from jax.experimental import pallas as pl
from jax.experimental.pallas import tpu as pltpu
from jax.sharding import PartitionSpec as P

N = 8
OFFS = (0, 1, -1, 2, -2, 3, -3, 4)
FOLD = 4
CAP = 4
ROWS = FOLD * CAP
MESH = pl.DeviceIdType.MESH
F32 = jnp.float32
BF16 = jnp.bfloat16
FAR = ((0, 1), (2, 3))
CHUNKS = ((0,), (1,), (2, 3), (4, 5), (6, 7))
ORDER = (
    (0, 0), (0, 1), (0, 2), (1, 0), (0, 3), (0, 4), (0, 5), (0, 6), (2, 0), (0, 7),
    (1, 1), (1, 2), (1, 3), (3, 0), (1, 4), (2, 1), (2, 3), (2, 2), (2, 4),
    (3, 3), (3, 4), (3, 1), (3, 2),
)
NEAR = (0, 1, 2, 3, 5, 6, 7)
VMEM_LIMIT = 32 * 1024 * 1024


def iota(shape, axis):
    return lax.broadcasted_iota(jnp.int32, shape, axis)


def routing(y, ids_ref, gw_ref, pick_ref, place_ref, pad):
    tok = ids_ref.shape[1]
    pad[...] = jnp.zeros_like(pad)
    pad[0:2, 0:tok] = ids_ref[...].astype(F32)
    pad[2:4, 0:tok] = pick_ref[...].astype(F32)
    pad[4:6, 0:tok] = gw_ref[...]
    pad[8:9, 0:N] = place_ref[...].astype(F32)
    wide = pad[0:8, :]
    wide = (
        wide
        + pltpu.roll(wide, tok, 1)
        + pltpu.roll(wide, 2 * tok, 1)
        + pltpu.roll(wide, 3 * tok, 1)
    )
    place_row = jnp.broadcast_to(pad[8:9, :], (N, 128))
    sub, lane = iota((N, 128), 0), iota((N, 128), 1)
    place_col = jnp.sum(jnp.where(sub == lane, place_row, 0.0), axis=1, keepdims=True)
    before = jnp.sum(
        jnp.where((place_row == place_col) & (lane < sub), 1.0, 0.0), axis=1, keepdims=True
    )
    subf = sub.astype(F32)
    row, col = iota((128, 128), 0), iota((128, 128), 1)
    j = row // ROWS
    offs = jnp.where(j % 2 == 1, (j + 1) // 2, -(j // 2))
    copy_of_row = ((y - offs + N) % N).astype(F32)
    chosen = []
    for k in range(2):
        match = place_col == wide[k : k + 1, :]
        copies = jnp.sum(jnp.where(match, 1.0, 0.0), axis=0, keepdims=True)
        wanted = jnp.where(copies > 1.5, wide[2 + k : 3 + k, :], 0.0)
        phys = jnp.sum(
            jnp.where(match & (before == wanted), subf, 0.0), axis=0, keepdims=True
        )
        chosen.append(jnp.where(copy_of_row == phys, 1.0, 0.0))
    earlier = jnp.where((row // tok == col // tok) & (row < col), 1.0, 0.0).astype(BF16)
    rank = jnp.dot((chosen[0] + chosen[1]).astype(BF16), earlier, preferred_element_type=F32)
    own = col // tok == (row // CAP) % FOLD
    slot = (row % CAP).astype(F32)
    in0 = jnp.where(own & (rank == slot), chosen[0], 0.0)
    in1 = jnp.where(own & (rank + chosen[0] == slot), chosen[1], 0.0)
    pick = (in0 + in1).astype(BF16)
    combine = in0 * wide[4:5, :] + in1 * wide[5:6, :]
    return pick, combine.T


def kernel(
    ids_hbm, gw_hbm, pick_hbm, place_hbm, tok_hbm, win_ref, wout_ref, out_ref,
    ids_ref, gw_ref, pick_ref, place_ref, tok_ref,
    pad, w1, w2, comb, ybuf, xbuf, xrows, xfar, part, pfar, sbuf, rbuf, obuf, cbuf, res,
    lsem, sent, ydr, agr, agl, rsr, rsl, yrr,
):
    wide = tok_ref.shape[1] // FOLD
    units = w2.shape[0]
    e = lax.axis_index("expert")
    y, z = e // N, e % N
    right = y * N + (z + 1) % N
    left = y * N + (z + N - 1) % N
    side = (right, left)

    barrier = pltpu.get_barrier_semaphore()
    peers = [(y + d) % N * N + z for d in (4, 3, 5, 2, 6, 1, 7)] + [right, left]
    for peer in peers:
        pl.semaphore_signal(barrier, inc=1, device_id={"expert": peer}, device_id_type=MESH)

    pairs = (
        (ids_hbm, ids_ref), (gw_hbm, gw_ref), (pick_hbm, pick_ref), (place_hbm, place_ref),
        (tok_hbm, tok_ref), (win_ref.at[0], w1.at[:, 0:units]),
        (win_ref.at[1], w1.at[:, units : 2 * units]), (wout_ref, w2),
    )
    loads = [pltpu.make_async_copy(src, dst, lsem.at[n]) for n, (src, dst) in enumerate(pairs)]
    for load in loads:
        load.start()
    for load in loads[:5]:
        load.wait()

    pick, combine = routing(y, ids_ref, gw_ref, pick_ref, place_ref, pad)
    tok_fold = jnp.concatenate(
        [tok_ref[:, q * wide : (q + 1) * wide] for q in range(FOLD)], axis=0
    )
    messages = jnp.dot(
        pick[:, : tok_fold.shape[0]], tok_fold, preferred_element_type=F32
    ).astype(BF16)
    ybuf[...] = messages
    xbuf[0, 0, 0:ROWS, :] = messages[0:ROWS]
    half_rows = combine[: tok_fold.shape[0]]
    high = half_rows.astype(BF16)
    comb[...] = jnp.concatenate([high, (half_rows - high.astype(F32)).astype(BF16)], axis=0)

    pl.semaphore_wait(barrier, len(peers))

    def remote(src, dst, send, recv, target):
        return pltpu.make_async_remote_copy(
            src_ref=src, dst_ref=dst, send_sem=send, recv_sem=recv,
            device_id={"expert": target}, device_id_type=MESH,
        )

    def msg(i, count=1):
        return slice(i * ROWS, (i + count) * ROWS)

    y_in = {}
    for j in range(1, N):
        y_in[j] = remote(
            ybuf.at[msg(j)], xbuf.at[j // 4, 0, msg(j % 4)], sent.at[0], ydr.at[j],
            (y - OFFS[j] + N) % N * N + z,
        )
        y_in[j].start()

    def hop(s, c, first, count, d):
        h, i = first // 4, first % 4
        src = (N - s) % N if d == 0 else s
        dst = N - 1 - s if d == 0 else s + 1
        return remote(
            xbuf.at[h, src, msg(i, count)], xbuf.at[h, dst, msg(i, count)], sent.at[1],
            agr.at[d, s, c] if s < 3 else agl.at[h, d], side[d],
        )

    def gather_one(s, n):
        if s == 0:
            if n > 0:
                y_in[n].wait_recv()
            chunk = [c for c in range(len(CHUNKS)) if n in CHUNKS[c]][0]
            for d in range(2):
                hop(0, chunk, n, 1, d).start()
            return
        first, count = CHUNKS[n][0], len(CHUNKS[n])
        for d in range(2):
            hop(s - 1, n, first, count, d).wait_recv()
            if s < 3 or first % 4 in FAR[d]:
                hop(s, n, first, count, d).start()

    def gather_last(h):
        for d in range(2):
            rows = xbuf.at[h, 4, msg(FAR[d][0], 2)]
            remote(rows, rows, sent.at[1], agl.at[h, d], side[d]).wait_recv()

    a, b = iota((4 * ROWS, 4 * ROWS), 0), iota((4 * ROWS, 4 * ROWS), 1)
    swap = jnp.where(
        (a // 16 == (b // 4) % 4) & ((a // 4) % 4 == b // 16) & (a % 4 == b % 4), 1.0, 0.0
    ).astype(BF16)

    def unfold(h, slot):
        rows = jnp.dot(swap, xbuf[h, slot], preferred_element_type=F32).astype(BF16)
        for q in range(FOLD):
            columns = slice(q * wide, (q + 1) * wide)
            if slot == 4:
                xfar[msg(h), columns] = rows[msg(q)]
            else:
                xrows[h, msg(NEAR.index(slot)), columns] = rows[msg(q)]

    def expert(rows, out):
        gate_up = jnp.dot(rows, w1[...], preferred_element_type=F32)
        gate = gate_up[:, :units]
        hidden = (gate / (1.0 + jnp.exp(-gate)) * gate_up[:, units:]).astype(BF16)
        for q in range(FOLD):
            out[q] = jnp.dot(
                hidden, w2[:, q * wide : (q + 1) * wide], preferred_element_type=F32
            )

    def partial_sum(h, slot, q):
        return pfar[q, msg(h), :] if slot == 4 else part[h, q, msg(NEAR.index(slot)), :]

    def ring(h, d, s, far):
        qs = FAR[d if far else 1 - d]
        at = 0 if s == 0 else 4 * s - 2 + qs[0]
        copy = remote(
            sbuf.at[h, d, at : at + 2], rbuf.at[h, d, at : at + 2], sent.at[2],
            rsl.at[h, d] if s == 3 else rsr.at[h, d, 2 * s - (0 if far else 1)], side[d],
        )
        return copy, at, qs

    def reduce_one(h, s, far):
        for d in range(2):
            copy, at, qs = ring(h, d, s, far)
            first = s == (0 if far else 1)
            if not first:
                arrived, back, _ = ring(h, d, s - 1, far)
                arrived.wait_recv()
            for n, q in enumerate(qs):
                value = partial_sum(h, 4 - s if d == 0 else 4 + s, q)
                if not first:
                    value = value + rbuf[h, d, back + n].astype(F32)
                sbuf[h, d, at + n] = value.astype(BF16)
            copy.start()

    def finish(h):
        for d in range(2):
            last = rbuf.at[h, d, 10:14]
            remote(last, last, sent.at[2], rsl.at[h, d], side[d]).wait_recv()
        sums = []
        for q in range(FOLD):
            value = partial_sum(h, 0, q)
            for d in range(2):
                value = value + rbuf[h, d, 10 + q].astype(F32)
            sums.append(value.astype(BF16))
        folded = jnp.dot(
            swap, jnp.concatenate(sums, axis=0), preferred_element_type=F32
        ).astype(BF16)
        obuf[msg(4 * h, 4)] = folded
        for i in reversed(range(4)):
            j = h * 4 + i
            if j == 0:
                cbuf[0:ROWS, :] = folded[0:ROWS]
                continue
            remote(
                obuf.at[msg(j)], cbuf.at[msg(j)], sent.at[3], yrr.at[0],
                (y + OFFS[j] + N) % N * N + z,
            ).start()

    waited = {}
    for s, n in ORDER:
        gather_one(s, n)
        h = n // 4 if s == 0 else CHUNKS[n][0] // 4
        waited[h, s] = waited.get((h, s), 0) + (1 if s == 0 else len(CHUNKS[n]))
        if waited[h, s] == 4:
            unfold(h, (N - s) % N)
            if s > 0:
                unfold(h, s)
    for load in loads[5:]:
        load.wait()
    for h in (1, 0):
        expert(xrows[h], part.at[h])
        reduce_one(h, 1, False)
    for h in (1, 0):
        gather_last(h)
        unfold(h, 4)
    expert(xfar[...], pfar)
    reduce_one(1, 0, True)
    reduce_one(0, 0, True)
    for s in range(1, 4):
        if s < 3:
            reduce_one(1, s + 1, False)
            reduce_one(0, s + 1, False)
        reduce_one(1, s, True)
        reduce_one(0, s, True)
    finish(1)
    finish(0)
    others = cbuf.at[ROWS : N * ROWS]
    remote(others, others, sent.at[3], yrr.at[0], right).wait_recv()
    both = jnp.dot(comb[...], cbuf[...], preferred_element_type=F32)
    half = both.shape[0] // 2
    result = both[:half] + both[half:]
    tok = tok_ref.shape[0]
    for q in range(FOLD):
        res[:, q * wide : (q + 1) * wide] = result[q * tok : (q + 1) * tok].astype(BF16)
    store = pltpu.make_async_copy(res, out_ref, lsem.at[0])
    store.start()
    for sem, whole in (
        (0, ybuf.at[ROWS : N * ROWS]), (1, xbuf.at[:, 0:7]), (2, sbuf), (3, obuf.at[ROWS : N * ROWS])
    ):
        remote(whole, whole, sent.at[sem], yrr.at[0], right).wait_send()
    store.wait()


def body(tokens, expert_ids, gate_weights, replica_pick, placement, w_in, w_out):
    tok, width = tokens.shape
    units = w_out.shape[0]
    wide = width // FOLD
    dma = pltpu.SemaphoreType.DMA
    operands = (
        expert_ids.T, gate_weights.T, replica_pick.T, placement.reshape(1, -1), tokens,
        w_in, w_out,
    )
    return pl.pallas_call(
        kernel,
        out_shape=jax.ShapeDtypeStruct((tok, width), BF16),
        in_specs=[pl.BlockSpec(memory_space=pl.ANY)] * 7,
        out_specs=pl.BlockSpec(memory_space=pl.ANY),
        scratch_shapes=[pltpu.VMEM(x.shape, x.dtype) for x in operands[:5]]
        + [
            pltpu.VMEM((16, 128), F32),
            pltpu.VMEM((width, 2 * units), BF16),
            pltpu.VMEM((units, width), BF16),
            pltpu.VMEM((2 * FOLD * tok, 128), BF16),
            pltpu.VMEM((N * ROWS, wide), BF16),
            pltpu.VMEM((2, N, 4 * ROWS, wide), BF16),
            pltpu.VMEM((2, 7 * ROWS, width), BF16),
            pltpu.VMEM((2 * ROWS, width), BF16),
            pltpu.VMEM((2, FOLD, 7 * ROWS, wide), F32),
            pltpu.VMEM((FOLD, 2 * ROWS, wide), F32),
            pltpu.VMEM((2, 2, 14, ROWS, wide), BF16),
            pltpu.VMEM((2, 2, 14, ROWS, wide), BF16),
            pltpu.VMEM((N * ROWS, wide), BF16),
            pltpu.VMEM((N * ROWS, wide), BF16),
            pltpu.VMEM((tok, width), BF16),
            dma((8,)),
            dma((4,)),
            dma((N,)),
            dma((2, 3, len(CHUNKS))),
            dma((2, 2)),
            dma((2, 2, 5)),
            dma((2, 2)),
            dma((1,)),
        ],
        compiler_params=pltpu.CompilerParams(
            collective_id=0, has_side_effects=True, vmem_limit_bytes=VMEM_LIMIT
        ),
    )(*[pltpu.with_memory_space_constraint(x, pltpu.HBM) for x in operands])


def solution(mesh):
    in_specs = (
        P(("dp", "expert"), None),
        P(("dp", "expert"), None),
        P(("dp", "expert"), None),
        P(("dp", "expert"), None),
        P(),
        P(None, None, "expert"),
        P("expert", None),
    )
    out_specs = P(("dp", "expert"), None)
    return jax.shard_map(body, mesh=mesh, in_specs=in_specs, out_specs=out_specs, check_vma=False)
```

time: 65.6 us -> 64.7 us (0.986)
  local copies, waits for them, and re-layouts: 1.55 us -> 0.65 us
    unnamed x1, local copies, waits for them, and re-layouts: 1.55 us -> 0.65 us
where the time goes in v3:
time: 64.7 us; the launch traced here: 64.6 us
  Pallas kernels  63.9 us (99%)
  local copies, waits for them, and re-layouts  0.65 us (1%)
    pallas_call x1, Pallas kernels, body(): pl.pallas_call(kernel, out_shape=jax.ShapeDtypeStruct((tok, width), BF16)...  63.9 us

profile of v3, /device:TPU:6, one launch (start us, length us, event | category | flops | bytes accessed | tf_op | source)
XLA Modules:
  0.0 64.6 jit_solution(11352662421502200257)
XLA Ops:
  0.0 63.9 %shard_map.73 = bf16[16,3584]{1,0:T(8,128)(2,1)S(1)} custom-call(s32[2,16]{1,0:T(2,128)} %bitcast.4, f32[2,16]{1,0:T(2,128)} %bitcast.5, s32[2,16]{1,0:T(2,128)} %bitcast.6, s32[1,8]{1,0:T(1,128)} %bitcast.7, bf16[16,3584]{1,0:T(8,128)(2,1)} %tok_hbm.1, bf16[2,3584,128]{2,1,0:T(8,128)(2,1)} %win_ref.1, bf16[128,3584]{1,0:T(8,128)(2,1)} %wout_ref.1), custom_call_target="tpu_custom_call" | custom-call | tf_op jit(solution)/shard_map/pallas_call | solution.py:295
  63.9 0.6 %copy.9 = bf16[16,3584]{1,0:T(8,128)(2,1)} copy(bf16[16,3584]{1,0:T(8,128)(2,1)S(1)} %shard_map.73) | data formatting | bytes 229376

commit v4 on v3

--- a/solution.py
+++ b/solution.py
@@ -16,13 +16,17 @@
 F32 = jnp.float32
 BF16 = jnp.bfloat16
 FAR = ((0, 1), (2, 3))
-CHUNKS = ((0,), (1,), (2, 3), (4, 5), (6, 7))
+BOTH = (0, 1)
 ORDER = (
-    (0, 0), (0, 1), (0, 2), (1, 0), (0, 3), (0, 4), (0, 5), (0, 6), (2, 0), (0, 7),
-    (1, 1), (1, 2), (1, 3), (3, 0), (1, 4), (2, 1), (2, 3), (2, 2), (2, 4),
-    (3, 3), (3, 4), (3, 1), (3, 2),
+    (0, 0, BOTH), (1, 0, BOTH), (0, 1, BOTH), (0, 2, BOTH), (0, 3, BOTH), (0, 4, BOTH),
+    (0, 5, BOTH), (0, 6, BOTH), (0, 7, BOTH), (1, 1, BOTH),
+    (1, 4, BOTH), (1, 5, BOTH), (1, 6, BOTH), (1, 7, BOTH), (1, 2, BOTH), (1, 3, BOTH),
+    (2, 4, BOTH), (2, 5, BOTH), (2, 6, BOTH), (2, 7, BOTH),
+    (2, 0, (0,)), (2, 2, (1,)), (2, 1, (0,)), (2, 3, (1,)),
+    (3, 4, (0,)), (3, 6, (1,)), (3, 5, (0,)), (3, 7, (1,)),
+    (2, 2, (0,)), (2, 0, (1,)), (2, 3, (0,)), (2, 1, (1,)),
+    (3, 0, (0,)), (3, 2, (1,)), (3, 1, (0,)), (3, 3, (1,)),
 )
-NEAR = (0, 1, 2, 3, 5, 6, 7)
 VMEM_LIMIT = 32 * 1024 * 1024
 
 
@@ -78,7 +82,7 @@
 def kernel(
     ids_hbm, gw_hbm, pick_hbm, place_hbm, tok_hbm, win_ref, wout_ref, out_ref,
     ids_ref, gw_ref, pick_ref, place_ref, tok_ref,
-    pad, w1, w2, comb, ybuf, xbuf, xrows, xfar, part, pfar, sbuf, rbuf, obuf, cbuf, res,
+    pad, w1, w2, comb, ybuf, xbuf, xrows, part, sbuf, rbuf, obuf, cbuf, res,
     lsem, sent, ydr, agr, agl, rsr, rsl, yrr,
 ):
     wide = tok_ref.shape[1] // FOLD
@@ -137,33 +141,32 @@
         )
         y_in[j].start()
 
-    def hop(s, c, first, count, d):
-        h, i = first // 4, first % 4
+    def hop(s, m, d):
+        h, i = m // 4, m % 4
         src = (N - s) % N if d == 0 else s
         dst = N - 1 - s if d == 0 else s + 1
+        if s < 2:
+            arrival = agr.at[d, 8 * s + m]
+        elif s == 2 and i in FAR[d]:
+            arrival = agr.at[d, 16 + 2 * h + i % 2]
+        else:
+            arrival = agl.at[h, d, s - 2]
         return remote(
-            xbuf.at[h, src, msg(i, count)], xbuf.at[h, dst, msg(i, count)], sent.at[1],
-            agr.at[d, s, c] if s < 3 else agl.at[h, d], side[d],
-        )
-
-    def gather_one(s, n):
-        if s == 0:
-            if n > 0:
-                y_in[n].wait_recv()
-            chunk = [c for c in range(len(CHUNKS)) if n in CHUNKS[c]][0]
-            for d in range(2):
-                hop(0, chunk, n, 1, d).start()
-            return
-        first, count = CHUNKS[n][0], len(CHUNKS[n])
-        for d in range(2):
-            hop(s - 1, n, first, count, d).wait_recv()
-            if s < 3 or first % 4 in FAR[d]:
-                hop(s, n, first, count, d).start()
+            xbuf.at[h, src, msg(i)], xbuf.at[h, dst, msg(i)], sent.at[1], arrival, side[d]
+        )
+
+    def gather_one(s, m, d):
+        if s > 0:
+            hop(s - 1, m, d).wait_recv()
+        hop(s, m, d).start()
 
     def gather_last(h):
         for d in range(2):
-            rows = xbuf.at[h, 4, msg(FAR[d][0], 2)]
-            remote(rows, rows, sent.at[1], agl.at[h, d], side[d]).wait_recv()
+            for slot, first in ((5 - 2 * d, FAR[1 - d][0]), (4, FAR[d][0])):
+                rows = xbuf.at[h, slot, msg(first, 2)]
+                remote(
+                    rows, rows, sent.at[1], agl.at[h, d, 1 if slot == 4 else 0], side[d]
+                ).wait_recv()
 
     a, b = iota((4 * ROWS, 4 * ROWS), 0), iota((4 * ROWS, 4 * ROWS), 1)
     swap = jnp.where(
@@ -173,11 +176,7 @@
     def unfold(h, slot):
         rows = jnp.dot(swap, xbuf[h, slot], preferred_element_type=F32).astype(BF16)
         for q in range(FOLD):
-            columns = slice(q * wide, (q + 1) * wide)
-            if slot == 4:
-                xfar[msg(h), columns] = rows[msg(q)]
-            else:
-                xrows[h, msg(NEAR.index(slot)), columns] = rows[msg(q)]
+            xrows[h, msg(slot), q * wide : (q + 1) * wide] = rows[msg(q)]
 
     def expert(rows, out):
         gate_up = jnp.dot(rows, w1[...], preferred_element_type=F32)
@@ -188,31 +187,31 @@
                 hidden, w2[:, q * wide : (q + 1) * wide], preferred_element_type=F32
             )
 
-    def partial_sum(h, slot, q):
-        return pfar[q, msg(h), :] if slot == 4 else part[h, q, msg(NEAR.index(slot)), :]
-
-    def ring(h, d, s, far):
-        qs = FAR[d if far else 1 - d]
-        at = 0 if s == 0 else 4 * s - 2 + qs[0]
+    def ring(h, d, s, q):
+        at = FAR[d].index(q) if s == 0 else 4 * s - 2 + q
         copy = remote(
-            sbuf.at[h, d, at : at + 2], rbuf.at[h, d, at : at + 2], sent.at[2],
-            rsl.at[h, d] if s == 3 else rsr.at[h, d, 2 * s - (0 if far else 1)], side[d],
-        )
-        return copy, at, qs
-
-    def reduce_one(h, s, far):
-        for d in range(2):
-            copy, at, qs = ring(h, d, s, far)
-            first = s == (0 if far else 1)
-            if not first:
-                arrived, back, _ = ring(h, d, s - 1, far)
-                arrived.wait_recv()
-            for n, q in enumerate(qs):
-                value = partial_sum(h, 4 - s if d == 0 else 4 + s, q)
-                if not first:
-                    value = value + rbuf[h, d, back + n].astype(F32)
-                sbuf[h, d, at + n] = value.astype(BF16)
-            copy.start()
+            sbuf.at[h, d, at], rbuf.at[h, d, at], sent.at[2],
+            rsl.at[h, d] if s == 3 else rsr.at[h, d, at], side[d],
+        )
+        return copy, at
+
+    def reduce_stage(h, stage):
+        for far in (True, False):
+            s = stage if far else stage + 1
+            if s > 3:
+                continue
+            for n in range(2):
+                for d in range(2):
+                    q = FAR[d if far else 1 - d][n]
+                    slot = 4 - s if d == 0 else 4 + s
+                    value = part[h, q, msg(slot), :]
+                    if stage > 0:
+                        arrived, back = ring(h, d, s - 1, q)
+                        arrived.wait_recv()
+                        value = value + rbuf[h, d, back].astype(F32)
+                    copy, at = ring(h, d, s, q)
+                    sbuf[h, d, at] = value.astype(BF16)
+                    copy.start()
 
     def finish(h):
         for d in range(2):
@@ -220,7 +219,7 @@
             remote(last, last, sent.at[2], rsl.at[h, d], side[d]).wait_recv()
         sums = []
         for q in range(FOLD):
-            value = partial_sum(h, 0, q)
+            value = part[h, q, 0:ROWS, :]
             for d in range(2):
                 value = value + rbuf[h, d, 10 + q].astype(F32)
             sums.append(value.astype(BF16))
@@ -239,31 +238,28 @@
             ).start()
 
     waited = {}
-    for s, n in ORDER:
-        gather_one(s, n)
-        h = n // 4 if s == 0 else CHUNKS[n][0] // 4
-        waited[h, s] = waited.get((h, s), 0) + (1 if s == 0 else len(CHUNKS[n]))
-        if waited[h, s] == 4:
-            unfold(h, (N - s) % N)
-            if s > 0:
-                unfold(h, s)
+    for s, m, directions in ORDER:
+        if s == 0 and m > 0:
+            y_in[m].wait_recv()
+        for d in directions:
+            gather_one(s, m, d)
+            if s == 0 and d == 1:
+                continue
+            key = m // 4, (N - s) % N if d == 0 else s
+            waited[key] = waited.get(key, 0) + 1
+            if waited[key] == 4:
+                unfold(*key)
     for load in loads[5:]:
         load.wait()
     for h in (1, 0):
+        gather_last(h)
+        for slot in (5, 3, 4):
+            unfold(h, slot)
         expert(xrows[h], part.at[h])
-        reduce_one(h, 1, False)
-    for h in (1, 0):
-        gather_last(h)
-        unfold(h, 4)
-    expert(xfar[...], pfar)
-    reduce_one(1, 0, True)
-    reduce_one(0, 0, True)
-    for s in range(1, 4):
-        if s < 3:
-            reduce_one(1, s + 1, False)
-            reduce_one(0, s + 1, False)
-        reduce_one(1, s, True)
-        reduce_one(0, s, True)
+        reduce_stage(h, 0)
+    for stage in range(1, 4):
+        reduce_stage(1, stage)
+        reduce_stage(0, stage)
     finish(1)
     finish(0)
     others = cbuf.at[ROWS : N * ROWS]
@@ -305,10 +301,8 @@
             pltpu.VMEM((2 * FOLD * tok, 128), BF16),
             pltpu.VMEM((N * ROWS, wide), BF16),
             pltpu.VMEM((2, N, 4 * ROWS, wide), BF16),
-            pltpu.VMEM((2, 7 * ROWS, width), BF16),
-            pltpu.VMEM((2 * ROWS, width), BF16),
-            pltpu.VMEM((2, FOLD, 7 * ROWS, wide), F32),
-            pltpu.VMEM((FOLD, 2 * ROWS, wide), F32),
+            pltpu.VMEM((2, N * ROWS, width), BF16),
+            pltpu.VMEM((2, FOLD, N * ROWS, wide), F32),
             pltpu.VMEM((2, 2, 14, ROWS, wide), BF16),
             pltpu.VMEM((2, 2, 14, ROWS, wide), BF16),
             pltpu.VMEM((N * ROWS, wide), BF16),
@@ -317,9 +311,9 @@
             dma((8,)),
             dma((4,)),
             dma((N,)),
-            dma((2, 3, len(CHUNKS))),
-            dma((2, 2)),
-            dma((2, 2, 5)),
+            dma((2, 20)),
+            dma((2, 2, 2)),
+            dma((2, 2, 10)),
             dma((2, 2)),
             dma((1,)),
         ],

time: 64.7 us -> 61.9 us (0.957)
  Pallas kernels: 63.9 us -> 61.1 us
    pallas_call x1, Pallas kernels: 63.9 us -> 61.1 us  [body(): pl.pallas_call(kernel, out_shape=jax.ShapeDtypeStruct((tok, width), BF16)...]
where the time goes in v4:
time: 61.9 us; the launch traced here: 61.8 us
  Pallas kernels  61.1 us (99%)
  local copies, waits for them, and re-layouts  0.65 us (1%)
    pallas_call x1, Pallas kernels, body(): pl.pallas_call(kernel, out_shape=jax.ShapeDtypeStruct((tok, width), BF16)...  61.1 us

profile of v4, /device:TPU:6, one launch (start us, length us, event | category | flops | bytes accessed | tf_op | source)
XLA Modules:
  0.0 61.8 jit_solution(17658384934464004782)
XLA Ops:
  0.0 61.1 %shard_map.73 = bf16[16,3584]{1,0:T(8,128)(2,1)S(1)} custom-call(s32[2,16]{1,0:T(2,128)} %bitcast.4, f32[2,16]{1,0:T(2,128)} %bitcast.5, s32[2,16]{1,0:T(2,128)} %bitcast.6, s32[1,8]{1,0:T(1,128)} %bitcast.7, bf16[16,3584]{1,0:T(8,128)(2,1)} %tok_hbm.1, bf16[2,3584,128]{2,1,0:T(8,128)(2,1)} %win_ref.1, bf16[128,3584]{1,0:T(8,128)(2,1)} %wout_ref.1), custom_call_target="tpu_custom_call" | custom-call | tf_op jit(solution)/shard_map/pallas_call | solution.py:291
  61.1 0.6 %copy.9 = bf16[16,3584]{1,0:T(8,128)(2,1)} copy(bf16[16,3584]{1,0:T(8,128)(2,1)S(1)} %shard_map.73) | data formatting | bytes 229376

commit v5 on v4

--- a/solution.py
+++ b/solution.py
@@ -1,5 +1,3 @@
-import functools
-
 import jax
 import jax.numpy as jnp
 from jax import lax
@@ -16,16 +14,31 @@
 F32 = jnp.float32
 BF16 = jnp.bfloat16
 FAR = ((0, 1), (2, 3))
-BOTH = (0, 1)
-ORDER = (
-    (0, 0, BOTH), (1, 0, BOTH), (0, 1, BOTH), (0, 2, BOTH), (0, 3, BOTH), (0, 4, BOTH),
-    (0, 5, BOTH), (0, 6, BOTH), (0, 7, BOTH), (1, 1, BOTH),
-    (1, 4, BOTH), (1, 5, BOTH), (1, 6, BOTH), (1, 7, BOTH), (1, 2, BOTH), (1, 3, BOTH),
-    (2, 4, BOTH), (2, 5, BOTH), (2, 6, BOTH), (2, 7, BOTH),
-    (2, 0, (0,)), (2, 2, (1,)), (2, 1, (0,)), (2, 3, (1,)),
-    (3, 4, (0,)), (3, 6, (1,)), (3, 5, (0,)), (3, 7, (1,)),
-    (2, 2, (0,)), (2, 0, (1,)), (2, 3, (0,)), (2, 1, (1,)),
-    (3, 0, (0,)), (3, 2, (1,)), (3, 1, (0,)), (3, 3, (1,)),
+RELAY, ARRIVED, HIDDEN, DOWN, SUM, FINISH = range(6)
+PROGRAM = (
+    (RELAY, 0, 0, 0), (RELAY, 0, 0, 1), (RELAY, 0, 1, 0), (RELAY, 0, 1, 1), (RELAY, 0, 2, 0),
+    (RELAY, 0, 2, 1), (RELAY, 1, 0, 1), (RELAY, 1, 0, 0), (RELAY, 0, 3, 0), (RELAY, 0, 3, 1),
+    (RELAY, 0, 4, 0), (RELAY, 0, 4, 1), (RELAY, 0, 5, 0), (RELAY, 0, 5, 1), (RELAY, 1, 1, 0),
+    (RELAY, 1, 1, 1), (RELAY, 0, 7, 0), (RELAY, 0, 7, 1), (RELAY, 1, 2, 0), (RELAY, 0, 6, 0),
+    (RELAY, 0, 6, 1), (RELAY, 1, 2, 1), (RELAY, 1, 4, 0), (RELAY, 1, 3, 1), (RELAY, 2, 0, 0),
+    (RELAY, 1, 5, 0), (RELAY, 1, 4, 1), (RELAY, 2, 0, 1), (RELAY, 1, 7, 1), (RELAY, 1, 3, 0),
+    (RELAY, 2, 1, 0), (RELAY, 1, 7, 0), (RELAY, 1, 6, 1), (RELAY, 2, 2, 1), (RELAY, 2, 3, 1),
+    (RELAY, 2, 4, 0), (RELAY, 1, 5, 1), (RELAY, 1, 6, 0), (RELAY, 2, 2, 0), (RELAY, 2, 5, 0),
+    (RELAY, 2, 1, 1), (RELAY, 2, 7, 1), (RELAY, 2, 6, 1), (RELAY, 3, 0, 0), (RELAY, 2, 3, 0),
+    (RELAY, 3, 2, 1), (RELAY, 3, 3, 1), (RELAY, 3, 1, 0), (RELAY, 2, 5, 1), (RELAY, 2, 6, 0),
+    (RELAY, 3, 4, 0), (RELAY, 2, 7, 0), (RELAY, 2, 4, 1), (RELAY, 3, 7, 1), (RELAY, 3, 5, 0),
+    (RELAY, 3, 6, 1), (ARRIVED, 0), (HIDDEN, 0), (DOWN, 0), (SUM, 0, 2, 1), (SUM, 0, 1, 0),
+    (SUM, 1, 3, 0), (SUM, 1, 1, 1), (SUM, 1, 0, 1), (SUM, 0, 0, 0), (SUM, 1, 2, 0), (SUM, 0, 3, 1),
+    (ARRIVED, 1), (HIDDEN, 1), (DOWN, 1), (SUM, 0, 7, 1), (SUM, 0, 4, 0), (SUM, 0, 5, 0),
+    (SUM, 0, 6, 1), (SUM, 1, 7, 0), (SUM, 1, 2, 1), (SUM, 1, 6, 0), (SUM, 1, 1, 0), (SUM, 2, 1, 1),
+    (SUM, 2, 3, 0), (SUM, 1, 4, 1), (SUM, 1, 5, 1), (SUM, 1, 7, 1), (SUM, 1, 4, 0), (SUM, 1, 3, 1),
+    (SUM, 1, 5, 0), (SUM, 2, 2, 0), (SUM, 1, 6, 1), (SUM, 2, 2, 1), (SUM, 1, 0, 0), (SUM, 2, 7, 0),
+    (SUM, 2, 1, 0), (SUM, 2, 4, 1), (SUM, 2, 6, 0), (SUM, 3, 3, 0), (SUM, 2, 5, 1), (SUM, 2, 7, 1),
+    (SUM, 2, 3, 1), (SUM, 2, 6, 1), (SUM, 2, 5, 0), (SUM, 3, 2, 1), (SUM, 2, 4, 0), (SUM, 2, 0, 0),
+    (SUM, 3, 4, 1), (SUM, 3, 5, 1), (SUM, 3, 7, 0), (SUM, 3, 7, 1), (SUM, 3, 6, 0), (SUM, 3, 2, 0),
+    (SUM, 3, 3, 1), (SUM, 3, 6, 1), (SUM, 3, 5, 0), (SUM, 3, 4, 0), (SUM, 3, 1, 0), (SUM, 2, 0, 1),
+    (SUM, 3, 1, 1), (FINISH, 7), (SUM, 3, 0, 0), (FINISH, 6), (FINISH, 5), (SUM, 3, 0, 1),
+    (FINISH, 4), (FINISH, 2), (FINISH, 3), (FINISH, 1), (FINISH, 0),
 )
 VMEM_LIMIT = 32 * 1024 * 1024
 
@@ -83,10 +96,10 @@
     ids_hbm, gw_hbm, pick_hbm, place_hbm, tok_hbm, win_ref, wout_ref, out_ref,
     ids_ref, gw_ref, pick_ref, place_ref, tok_ref,
     pad, w1, w2, comb, ybuf, xbuf, xrows, part, sbuf, rbuf, obuf, cbuf, res,
-    lsem, sent, ydr, agr, agl, rsr, rsl, yrr,
+    lsem, sent, ydr, agr, agl, rsr, yrr,
 ):
     wide = tok_ref.shape[1] // FOLD
-    units = w2.shape[0]
+    units = wout_ref.shape[0]
     e = lax.axis_index("expert")
     y, z = e // N, e % N
     right = y * N + (z + 1) % N
@@ -101,7 +114,10 @@
     pairs = (
         (ids_hbm, ids_ref), (gw_hbm, gw_ref), (pick_hbm, pick_ref), (place_hbm, place_ref),
         (tok_hbm, tok_ref), (win_ref.at[0], w1.at[:, 0:units]),
-        (win_ref.at[1], w1.at[:, units : 2 * units]), (wout_ref, w2),
+        (win_ref.at[1], w1.at[:, units : 2 * units]),
+    ) + tuple(
+        (wout_ref.at[:, q * wide : (q + 1) * wide], w2.at[q // 2, q % 2 * units : (q % 2 + 1) * units])
+        for q in range(FOLD)
     )
     loads = [pltpu.make_async_copy(src, dst, lsem.at[n]) for n, (src, dst) in enumerate(pairs)]
     for load in loads:
@@ -155,18 +171,29 @@
             xbuf.at[h, src, msg(i)], xbuf.at[h, dst, msg(i)], sent.at[1], arrival, side[d]
         )
 
-    def gather_one(s, m, d):
+    waited = {}
+
+    def relay(s, m, d):
         if s > 0:
             hop(s - 1, m, d).wait_recv()
+        elif d == 0 and m > 0:
+            y_in[m].wait_recv()
         hop(s, m, d).start()
-
-    def gather_last(h):
+        if s > 0 or d == 0:
+            key = m // 4, (N - s) % N if d == 0 else s
+            waited[key] = waited.get(key, 0) + 1
+            if waited[key] == 4:
+                unfold(*key)
+
+    def arrived(h):
         for d in range(2):
             for slot, first in ((5 - 2 * d, FAR[1 - d][0]), (4, FAR[d][0])):
                 rows = xbuf.at[h, slot, msg(first, 2)]
                 remote(
                     rows, rows, sent.at[1], agl.at[h, d, 1 if slot == 4 else 0], side[d]
                 ).wait_recv()
+        for slot in (5, 3, 4):
+            unfold(h, slot)
 
     a, b = iota((4 * ROWS, 4 * ROWS), 0), iota((4 * ROWS, 4 * ROWS), 1)
     swap = jnp.where(
@@ -178,90 +205,72 @@
         for q in range(FOLD):
             xrows[h, msg(slot), q * wide : (q + 1) * wide] = rows[msg(q)]
 
-    def expert(rows, out):
-        gate_up = jnp.dot(rows, w1[...], preferred_element_type=F32)
+    hidden = {}
+
+    def hidden_of(h):
+        gate_up = jnp.dot(xrows[h], w1[...], preferred_element_type=F32)
         gate = gate_up[:, :units]
-        hidden = (gate / (1.0 + jnp.exp(-gate)) * gate_up[:, units:]).astype(BF16)
-        for q in range(FOLD):
-            out[q] = jnp.dot(
-                hidden, w2[:, q * wide : (q + 1) * wide], preferred_element_type=F32
-            )
-
-    def ring(h, d, s, q):
-        at = FAR[d].index(q) if s == 0 else 4 * s - 2 + q
+        act = (gate / (1.0 + jnp.exp(-gate)) * gate_up[:, units:]).astype(BF16)
+        rows = act.shape[0]
+        r, c = iota((2 * rows, rows), 0), iota((2 * rows, rows), 1)
+        twice = jnp.where((r // 8 == c // 4) & (r % 4 == c % 4), 1.0, 0.0).astype(BF16)
+        spread = jnp.dot(twice, act, preferred_element_type=F32)
+        odd = iota(spread.shape, 0) // 4 % 2 == 1
+        hidden[h] = jnp.concatenate(
+            [jnp.where(odd, 0.0, spread), jnp.where(odd, spread, 0.0)], axis=1
+        ).astype(BF16)
+
+    def down(h):
+        for pair in range(2):
+            part[h, pair] = jnp.dot(hidden[h], w2[pair], preferred_element_type=F32)
+
+    def partial_sum(m, slot):
+        rows = slice(32 * slot + 8 * (m % 4), 32 * slot + 8 * (m % 4) + 8)
+        return jnp.concatenate([part[m // 4, 0, rows, :], part[m // 4, 1, rows, :]], axis=0)
+
+    def ring(d, s, m):
+        if m % 4 in FAR[d]:
+            at = 4 * s + 2 * (m // 4) + m % 2
+        else:
+            at = 12 + 4 * s + 2 * (m // 4) + m % 2
         copy = remote(
-            sbuf.at[h, d, at], rbuf.at[h, d, at], sent.at[2],
-            rsl.at[h, d] if s == 3 else rsr.at[h, d, at], side[d],
+            sbuf.at[d, at], rbuf.at[d, at], sent.at[2], rsr.at[d, at], side[d]
         )
         return copy, at
 
-    def reduce_stage(h, stage):
-        for far in (True, False):
-            s = stage if far else stage + 1
-            if s > 3:
-                continue
-            for n in range(2):
-                for d in range(2):
-                    q = FAR[d if far else 1 - d][n]
-                    slot = 4 - s if d == 0 else 4 + s
-                    value = part[h, q, msg(slot), :]
-                    if stage > 0:
-                        arrived, back = ring(h, d, s - 1, q)
-                        arrived.wait_recv()
-                        value = value + rbuf[h, d, back].astype(F32)
-                    copy, at = ring(h, d, s, q)
-                    sbuf[h, d, at] = value.astype(BF16)
-                    copy.start()
-
-    def finish(h):
+    def add_on(s, m, d):
+        value = partial_sum(m, 4 - s if d == 0 else 4 + s)
+        if s > (0 if m % 4 in FAR[d] else 1):
+            earlier, at = ring(d, s - 1, m)
+            earlier.wait_recv()
+            value = value + rbuf[d, at].astype(F32)
+        copy, at = ring(d, s, m)
+        sbuf[d, at] = value.astype(BF16)
+        copy.start()
+
+    def finish(m):
+        value = partial_sum(m, 0)
         for d in range(2):
-            last = rbuf.at[h, d, 10:14]
-            remote(last, last, sent.at[2], rsl.at[h, d], side[d]).wait_recv()
-        sums = []
-        for q in range(FOLD):
-            value = part[h, q, 0:ROWS, :]
-            for d in range(2):
-                value = value + rbuf[h, d, 10 + q].astype(F32)
-            sums.append(value.astype(BF16))
-        folded = jnp.dot(
-            swap, jnp.concatenate(sums, axis=0), preferred_element_type=F32
-        ).astype(BF16)
-        obuf[msg(4 * h, 4)] = folded
-        for i in reversed(range(4)):
-            j = h * 4 + i
-            if j == 0:
-                cbuf[0:ROWS, :] = folded[0:ROWS]
-                continue
-            remote(
-                obuf.at[msg(j)], cbuf.at[msg(j)], sent.at[3], yrr.at[0],
-                (y + OFFS[j] + N) % N * N + z,
-            ).start()
-
-    waited = {}
-    for s, m, directions in ORDER:
-        if s == 0 and m > 0:
-            y_in[m].wait_recv()
-        for d in directions:
-            gather_one(s, m, d)
-            if s == 0 and d == 1:
-                continue
-            key = m // 4, (N - s) % N if d == 0 else s
-            waited[key] = waited.get(key, 0) + 1
-            if waited[key] == 4:
-                unfold(*key)
-    for load in loads[5:]:
-        load.wait()
-    for h in (1, 0):
-        gather_last(h)
-        for slot in (5, 3, 4):
-            unfold(h, slot)
-        expert(xrows[h], part.at[h])
-        reduce_stage(h, 0)
-    for stage in range(1, 4):
-        reduce_stage(1, stage)
-        reduce_stage(0, stage)
-    finish(1)
-    finish(0)
+            last, at = ring(d, 3, m)
+            last.wait_recv()
+            value = value + rbuf[d, at].astype(F32)
+        if m == 0:
+            cbuf[0:ROWS, :] = value.astype(BF16)
+            return
+        obuf[msg(m)] = value.astype(BF16)
+        remote(
+            obuf.at[msg(m)], cbuf.at[msg(m)], sent.at[3], yrr.at[0],
+            (y + OFFS[m] + N) % N * N + z,
+        ).start()
+
+    steps = {
+        RELAY: relay, ARRIVED: arrived, HIDDEN: hidden_of, DOWN: down, SUM: add_on, FINISH: finish
+    }
+    for kind, *which in PROGRAM:
+        if kind == HIDDEN and not hidden:
+            for load in loads[5:]:
+                load.wait()
+        steps[kind](*which)
     others = cbuf.at[ROWS : N * ROWS]
     remote(others, others, sent.at[3], yrr.at[0], right).wait_recv()
     both = jnp.dot(comb[...], cbuf[...], preferred_element_type=F32)
@@ -297,24 +306,23 @@
         + [
             pltpu.VMEM((16, 128), F32),
             pltpu.VMEM((width, 2 * units), BF16),
-            pltpu.VMEM((units, width), BF16),
+            pltpu.VMEM((2, 2 * units, wide), BF16),
             pltpu.VMEM((2 * FOLD * tok, 128), BF16),
             pltpu.VMEM((N * ROWS, wide), BF16),
             pltpu.VMEM((2, N, 4 * ROWS, wide), BF16),
             pltpu.VMEM((2, N * ROWS, width), BF16),
-            pltpu.VMEM((2, FOLD, N * ROWS, wide), F32),
-            pltpu.VMEM((2, 2, 14, ROWS, wide), BF16),
-            pltpu.VMEM((2, 2, 14, ROWS, wide), BF16),
+            pltpu.VMEM((2, 2, 2 * N * ROWS, wide), F32),
+            pltpu.VMEM((2, 28, ROWS, wide), BF16),
+            pltpu.VMEM((2, 28, ROWS, wide), BF16),
             pltpu.VMEM((N * ROWS, wide), BF16),
             pltpu.VMEM((N * ROWS, wide), BF16),
             pltpu.VMEM((tok, width), BF16),
-            dma((8,)),
+            dma((11,)),
             dma((4,)),
             dma((N,)),
             dma((2, 20)),
             dma((2, 2, 2)),
-            dma((2, 2, 10)),
-            dma((2, 2)),
+            dma((2, 28)),
             dma((1,)),
         ],
         compiler_params=pltpu.CompilerParams(

time: 61.9 us -> 61.6 us (level)
  no operation moved by 1% of the time
where the time goes in v5:
time: 61.6 us; the launch traced here: 61.4 us
  Pallas kernels  60.8 us (99%)
  local copies, waits for them, and re-layouts  0.65 us (1%)
    pallas_call x1, Pallas kernels, body(): pl.pallas_call(kernel, out_shape=jax.ShapeDtypeStruct((tok, width), BF16)...  60.8 us

profile of v5, /device:TPU:6, one launch (start us, length us, event | category | flops | bytes accessed | tf_op | source)
XLA Modules:
  0.0 61.4 jit_solution(2356218067603444128)
XLA Ops:
  0.0 60.8 %shard_map.73 = bf16[16,3584]{1,0:T(8,128)(2,1)S(1)} custom-call(s32[2,16]{1,0:T(2,128)} %bitcast.4, f32[2,16]{1,0:T(2,128)} %bitcast.5, s32[2,16]{1,0:T(2,128)} %bitcast.6, s32[1,8]{1,0:T(1,128)} %bitcast.7, bf16[16,3584]{1,0:T(8,128)(2,1)} %tok_hbm.1, bf16[2,3584,128]{2,1,0:T(8,128)(2,1)} %win_ref.1, bf16[128,3584]{1,0:T(8,128)(2,1)} %wout_ref.1), custom_call_target="tpu_custom_call" | custom-call | tf_op jit(solution)/shard_map/pallas_call | solution.py:300
  60.8 0.6 %copy.9 = bf16[16,3584]{1,0:T(8,128)(2,1)} copy(bf16[16,3584]{1,0:T(8,128)(2,1)S(1)} %shard_map.73) | data formatting | bytes 229376

commit v6 on v5

--- a/solution.py
+++ b/solution.py
@@ -14,7 +14,7 @@
 F32 = jnp.float32
 BF16 = jnp.bfloat16
 FAR = ((0, 1), (2, 3))
-RELAY, ARRIVED, HIDDEN, DOWN, SUM, FINISH = range(6)
+RELAY, ARRIVED, EARLY, LATE, SUM, FINISH = range(6)
 PROGRAM = (
     (RELAY, 0, 0, 0), (RELAY, 0, 0, 1), (RELAY, 0, 1, 0), (RELAY, 0, 1, 1), (RELAY, 0, 2, 0),
     (RELAY, 0, 2, 1), (RELAY, 1, 0, 1), (RELAY, 1, 0, 0), (RELAY, 0, 3, 0), (RELAY, 0, 3, 1),
@@ -27,9 +27,9 @@
     (RELAY, 2, 1, 1), (RELAY, 2, 7, 1), (RELAY, 2, 6, 1), (RELAY, 3, 0, 0), (RELAY, 2, 3, 0),
     (RELAY, 3, 2, 1), (RELAY, 3, 3, 1), (RELAY, 3, 1, 0), (RELAY, 2, 5, 1), (RELAY, 2, 6, 0),
     (RELAY, 3, 4, 0), (RELAY, 2, 7, 0), (RELAY, 2, 4, 1), (RELAY, 3, 7, 1), (RELAY, 3, 5, 0),
-    (RELAY, 3, 6, 1), (ARRIVED, 0), (HIDDEN, 0), (DOWN, 0), (SUM, 0, 2, 1), (SUM, 0, 1, 0),
+    (RELAY, 3, 6, 1), (EARLY, 0), (ARRIVED, 0), (LATE, 0), (SUM, 0, 2, 1), (SUM, 0, 1, 0),
     (SUM, 1, 3, 0), (SUM, 1, 1, 1), (SUM, 1, 0, 1), (SUM, 0, 0, 0), (SUM, 1, 2, 0), (SUM, 0, 3, 1),
-    (ARRIVED, 1), (HIDDEN, 1), (DOWN, 1), (SUM, 0, 7, 1), (SUM, 0, 4, 0), (SUM, 0, 5, 0),
+    (EARLY, 1), (ARRIVED, 1), (LATE, 1), (SUM, 0, 7, 1), (SUM, 0, 4, 0), (SUM, 0, 5, 0),
     (SUM, 0, 6, 1), (SUM, 1, 7, 0), (SUM, 1, 2, 1), (SUM, 1, 6, 0), (SUM, 1, 1, 0), (SUM, 2, 1, 1),
     (SUM, 2, 3, 0), (SUM, 1, 4, 1), (SUM, 1, 5, 1), (SUM, 1, 7, 1), (SUM, 1, 4, 0), (SUM, 1, 3, 1),
     (SUM, 1, 5, 0), (SUM, 2, 2, 0), (SUM, 1, 6, 1), (SUM, 2, 2, 1), (SUM, 1, 0, 0), (SUM, 2, 7, 0),
@@ -40,6 +40,9 @@
     (SUM, 3, 1, 1), (FINISH, 7), (SUM, 3, 0, 0), (FINISH, 6), (FINISH, 5), (SUM, 3, 0, 1),
     (FINISH, 4), (FINISH, 2), (FINISH, 3), (FINISH, 1), (FINISH, 0),
 )
+PLACE = (0, 1, 2, 5, 6, 7, 3, 4)
+NEARER = 5
+SPARE = (tuple(range(14)), tuple(range(12)) + (14, 15))
 VMEM_LIMIT = 32 * 1024 * 1024
 
 
@@ -203,29 +206,40 @@
     def unfold(h, slot):
         rows = jnp.dot(swap, xbuf[h, slot], preferred_element_type=F32).astype(BF16)
         for q in range(FOLD):
-            xrows[h, msg(slot), q * wide : (q + 1) * wide] = rows[msg(q)]
-
-    hidden = {}
-
-    def hidden_of(h):
-        gate_up = jnp.dot(xrows[h], w1[...], preferred_element_type=F32)
+            xrows[h, msg(PLACE[slot]), q * wide : (q + 1) * wide] = rows[msg(q)]
+
+    def expert(h, low, high):
+        gate_up = jnp.dot(xrows[h, low:high], w1[...], preferred_element_type=F32)
         gate = gate_up[:, :units]
         act = (gate / (1.0 + jnp.exp(-gate)) * gate_up[:, units:]).astype(BF16)
-        rows = act.shape[0]
+        rows = high - low
         r, c = iota((2 * rows, rows), 0), iota((2 * rows, rows), 1)
         twice = jnp.where((r // 8 == c // 4) & (r % 4 == c % 4), 1.0, 0.0).astype(BF16)
         spread = jnp.dot(twice, act, preferred_element_type=F32)
         odd = iota(spread.shape, 0) // 4 % 2 == 1
-        hidden[h] = jnp.concatenate(
+        hidden = jnp.concatenate(
             [jnp.where(odd, 0.0, spread), jnp.where(odd, spread, 0.0)], axis=1
         ).astype(BF16)
-
-    def down(h):
         for pair in range(2):
-            part[h, pair] = jnp.dot(hidden[h], w2[pair], preferred_element_type=F32)
+            part[h, pair, 2 * low : 2 * high] = jnp.dot(
+                hidden, w2[pair], preferred_element_type=F32
+            )
+
+    loaded = []
+
+    def early(h):
+        if not loaded:
+            for load in loads[5:]:
+                load.wait()
+            loaded.append(h)
+        expert(h, 0, NEARER * ROWS)
+
+    def late(h):
+        expert(h, NEARER * ROWS, N * ROWS)
 
     def partial_sum(m, slot):
-        rows = slice(32 * slot + 8 * (m % 4), 32 * slot + 8 * (m % 4) + 8)
+        first = 32 * PLACE[slot] + 8 * (m % 4)
+        rows = slice(first, first + 8)
         return jnp.concatenate([part[m // 4, 0, rows, :], part[m // 4, 1, rows, :]], axis=0)
 
     def ring(d, s, m):
@@ -233,9 +247,9 @@
             at = 4 * s + 2 * (m // 4) + m % 2
         else:
             at = 12 + 4 * s + 2 * (m // 4) + m % 2
-        copy = remote(
-            sbuf.at[d, at], rbuf.at[d, at], sent.at[2], rsr.at[d, at], side[d]
-        )
+        spare = len(SPARE[d])
+        arrival = agr.at[d, SPARE[d][at]] if at < spare else rsr.at[d, at - spare]
+        copy = remote(sbuf.at[d, at], rbuf.at[d, at], sent.at[2], arrival, side[d])
         return copy, at
 
     def add_on(s, m, d):
@@ -264,12 +278,9 @@
         ).start()
 
     steps = {
-        RELAY: relay, ARRIVED: arrived, HIDDEN: hidden_of, DOWN: down, SUM: add_on, FINISH: finish
+        RELAY: relay, ARRIVED: arrived, EARLY: early, LATE: late, SUM: add_on, FINISH: finish
     }
     for kind, *which in PROGRAM:
-        if kind == HIDDEN and not hidden:
-            for load in loads[5:]:
-                load.wait()
         steps[kind](*which)
     others = cbuf.at[ROWS : N * ROWS]
     remote(others, others, sent.at[3], yrr.at[0], right).wait_recv()
@@ -322,7 +333,7 @@
             dma((N,)),
             dma((2, 20)),
             dma((2, 2, 2)),
-            dma((2, 28)),
+            dma((2, 14)),
             dma((1,)),
         ],
         compiler_params=pltpu.CompilerParams(

time: 61.6 us -> 61.4 us (level)
  no operation moved by 1% of the time
where the time goes in v6:
time: 61.4 us; the launch traced here: 61.3 us
  Pallas kernels  60.6 us (99%)
  local copies, waits for them, and re-layouts  0.65 us (1%)
    pallas_call x1, Pallas kernels, body(): pl.pallas_call(kernel, out_shape=jax.ShapeDtypeStruct((tok, width), BF16)...  60.6 us

profile of v6, /device:TPU:6, one launch (start us, length us, event | category | flops | bytes accessed | tf_op | source)
XLA Modules:
  0.0 61.3 jit_solution(147519297978356964)
XLA Ops:
  0.0 60.6 %shard_map.73 = bf16[16,3584]{1,0:T(8,128)(2,1)S(1)} custom-call(s32[2,16]{1,0:T(2,128)} %bitcast.4, f32[2,16]{1,0:T(2,128)} %bitcast.5, s32[2,16]{1,0:T(2,128)} %bitcast.6, s32[1,8]{1,0:T(1,128)} %bitcast.7, bf16[16,3584]{1,0:T(8,128)(2,1)} %tok_hbm.1, bf16[2,3584,128]{2,1,0:T(8,128)(2,1)} %win_ref.1, bf16[128,3584]{1,0:T(8,128)(2,1)} %wout_ref.1), custom_call_target="tpu_custom_call" | custom-call | tf_op jit(solution)/shard_map/pallas_call | solution.py:311
  60.7 0.6 %copy.9 = bf16[16,3584]{1,0:T(8,128)(2,1)} copy(bf16[16,3584]{1,0:T(8,128)(2,1)S(1)} %shard_map.73) | data formatting | bytes 229376

commit v7 on v6

--- a/solution.py
+++ b/solution.py
@@ -36,8 +36,8 @@
     (SUM, 2, 1, 0), (SUM, 2, 4, 1), (SUM, 2, 6, 0), (SUM, 3, 3, 0), (SUM, 2, 5, 1), (SUM, 2, 7, 1),
     (SUM, 2, 3, 1), (SUM, 2, 6, 1), (SUM, 2, 5, 0), (SUM, 3, 2, 1), (SUM, 2, 4, 0), (SUM, 2, 0, 0),
     (SUM, 3, 4, 1), (SUM, 3, 5, 1), (SUM, 3, 7, 0), (SUM, 3, 7, 1), (SUM, 3, 6, 0), (SUM, 3, 2, 0),
-    (SUM, 3, 3, 1), (SUM, 3, 6, 1), (SUM, 3, 5, 0), (SUM, 3, 4, 0), (SUM, 3, 1, 0), (SUM, 2, 0, 1),
-    (SUM, 3, 1, 1), (FINISH, 7), (SUM, 3, 0, 0), (FINISH, 6), (FINISH, 5), (SUM, 3, 0, 1),
+    (SUM, 3, 3, 1), (SUM, 3, 6, 1), (SUM, 2, 0, 1), (SUM, 3, 5, 0), (SUM, 3, 4, 0), (SUM, 3, 1, 0),
+    (SUM, 3, 1, 1), (SUM, 3, 0, 0), (FINISH, 7), (FINISH, 6), (SUM, 3, 0, 1), (FINISH, 5),
     (FINISH, 4), (FINISH, 2), (FINISH, 3), (FINISH, 1), (FINISH, 0),
 )
 PLACE = (0, 1, 2, 5, 6, 7, 3, 4)

time: 61.4 us -> 61.5 us (level)
  no operation moved by 1% of the time
where the time goes in v7:
time: 61.5 us; the launch traced here: 61.4 us
  Pallas kernels  60.7 us (99%)
  local copies, waits for them, and re-layouts  0.65 us (1%)
    pallas_call x1, Pallas kernels, body(): pl.pallas_call(kernel, out_shape=jax.ShapeDtypeStruct((tok, width), BF16)...  60.7 us

profile of v7, /device:TPU:6, one launch (start us, length us, event | category | flops | bytes accessed | tf_op | source)
XLA Modules:
  0.0 61.4 jit_solution(15554470200953497046)
XLA Ops:
  0.0 60.7 %shard_map.73 = bf16[16,3584]{1,0:T(8,128)(2,1)S(1)} custom-call(s32[2,16]{1,0:T(2,128)} %bitcast.4, f32[2,16]{1,0:T(2,128)} %bitcast.5, s32[2,16]{1,0:T(2,128)} %bitcast.6, s32[1,8]{1,0:T(1,128)} %bitcast.7, bf16[16,3584]{1,0:T(8,128)(2,1)} %tok_hbm.1, bf16[2,3584,128]{2,1,0:T(8,128)(2,1)} %win_ref.1, bf16[128,3584]{1,0:T(8,128)(2,1)} %wout_ref.1), custom_call_target="tpu_custom_call" | custom-call | tf_op jit(solution)/shard_map/pallas_call | solution.py:311
  60.7 0.6 %copy.9 = bf16[16,3584]{1,0:T(8,128)(2,1)} copy(bf16[16,3584]{1,0:T(8,128)(2,1)S(1)} %shard_map.73) | data formatting | bytes 229376
